TPU v7x, 32 devices: a whole 2x2x4 slice. The times are simulated.
32 devices in a mesh: row: 1, voc: 32 (over z, y, x, core).
Axes of the slice: x: 2, y: 2, z: 4, core: 2. Of those that a mesh axis runs over, the one named last changes fastest.
Arguments:
- hidden_states: bfloat16 [256, 4096], P('row'), may hold values from -72 to 72
- student_head: bfloat16 [4096, 65536], P('row', 'voc'), may hold values from -2 to 2
- teacher_probs: bfloat16 [256, 81920], P('row', 'voc'), may hold values from 9.9658966e-05 to 1
- block_map: int32 [512, 2], replicated, may hold values from 0 to 639, as said below
- context: int32 [4], P('row'), may hold values from 0 to 3
- map_gates: float32 [4, 512, 2], P(None, 'voc'), may hold values from 0.2 to 5
- map_tiles: bfloat16 [512, 2, 128, 128], P('voc'), may hold values from 0.0009994507 to 1
Outputs:
- grad_logits: bfloat16 [256, 65536], P('row', 'voc')
- head_grad: bfloat16 [4096, 65536], P('row', 'voc')
- kl_loss: float32 [], replicated
Inputs may be any that keep to these rules, and one draw needn't show every extreme that they name: `block_map`: in each aligned block of 16 student blocks, at most 2 of the 32 listed ids lie in any one aligned range of 20 teacher blocks, and exactly 2 in one such range.
All inputs are finite; a program needn't handle non-finite values.
Results may differ from a plain program's by a relative error of at most 0.013.
Values may be sent and summed in bfloat16 or wider, within the bound.
A program may use at most 128 MiB of HBM per device.

v0:
```python
import math

import jax
import jax.numpy as jnp
from jax import lax
from jax.sharding import PartitionSpec as P


def map_teacher(teacher_probs, block_map, context, map_gates, map_tiles):
    voc_count = lax.axis_size("voc")
    own_index = lax.axis_index("voc")
    blocks, fanout, block_width, _ = map_tiles.shape
    tokens_here = teacher_probs.shape[0]
    per_shard = teacher_probs.shape[1] // block_width
    entries = blocks * fanout
    capacity = entries // voc_count + 1
    wanted_all = block_map.reshape(voc_count, entries)
    sources_all = wanted_all // per_shard
    owned = (sources_all == own_index).astype(jnp.int32)
    rank_in = jnp.cumsum(owned, axis=1) - 1
    selected = owned[:, None, :] * (
        rank_in[:, None, :] == jnp.arange(capacity)[None, :, None]
    ).astype(jnp.int32)
    local_ids = wanted_all - own_index * per_shard
    take_index = jnp.sum(selected * local_ids[:, None, :], axis=2).reshape(-1)
    filled = jnp.sum(selected, axis=2).reshape(-1) > 0
    teacher_blocks = teacher_probs.reshape(tokens_here, per_shard, block_width)
    outgoing = jnp.where(
        filled[None, :, None],
        jnp.take(teacher_blocks, take_index, axis=1),
        jnp.zeros((), teacher_probs.dtype),
    )
    incoming = lax.all_to_all(outgoing, "voc", split_axis=1, concat_axis=1, tiled=True)
    wanted = lax.dynamic_index_in_dim(wanted_all, own_index, 0, keepdims=False)
    sources = wanted // per_shard
    source_hot = (sources[:, None] == jnp.arange(voc_count)[None, :]).astype(jnp.int32)
    position = jnp.sum(source_hot * (jnp.cumsum(source_hot, axis=0) - 1), axis=1)
    pieces = jnp.take(incoming, sources * capacity + position, axis=1).reshape(
        tokens_here, blocks, fanout, block_width
    )
    products = jnp.einsum("tbkj,bkjc->tbkc", pieces, map_tiles, preferred_element_type=jnp.float32)
    window = tokens_here // context.shape[0]
    token_context = jnp.repeat(context, window)
    context_count = map_gates.shape[0]
    context_hot = (token_context[:, None] == jnp.arange(context_count)[None, :]).astype(jnp.float32)
    gate_token = jnp.dot(
        context_hot, map_gates.reshape(context_count, entries), precision=lax.Precision.HIGHEST
    )
    gate_token = gate_token.reshape(tokens_here, blocks, fanout)
    mapped = jnp.sum(gate_token[..., None] * products, axis=2)
    return mapped.reshape(tokens_here, blocks * block_width)


def per_device(
    hidden_states, student_head, teacher_probs, block_map, context, map_gates, map_tiles
):
    tokens_here = hidden_states.shape[0]
    vocab_cols = student_head.shape[1]
    rows_total = tokens_here * lax.axis_size("row")
    inv_root = 1.0 / math.sqrt(rows_total)
    columns = hidden_states
    logits = jnp.dot(
        columns,
        lax.all_gather(student_head, "row", axis=0, tiled=True),
        preferred_element_type=jnp.float32,
    )
    mapped = map_teacher(teacher_probs, block_map, context, map_gates, map_tiles)
    local_total = jnp.sum(mapped, axis=1)
    peak = lax.pmax(jnp.max(logits, axis=1), "voc")
    summed, row_total = lax.psum(
        (jnp.sum(jnp.exp(logits - peak[:, None]), axis=1), local_total), "voc"
    )
    log_norm = peak + jnp.log(summed)
    target = mapped / row_total[:, None]
    vocab_total = vocab_cols * lax.axis_size("voc")
    grad_logits = (vocab_total * (jnp.exp(logits - log_norm[:, None]) - target)).astype(
        jnp.bfloat16
    )
    kl_partial = jnp.sum(target * (jnp.log(target) - logits + log_norm[:, None]))
    kl_loss = lax.psum(kl_partial, ("row", "voc")) / rows_total
    columns = hidden_states
    head_grad = lax.psum_scatter(
        (
            jnp.einsum("td,tv->dv", columns, grad_logits, preferred_element_type=jnp.float32)
            * inv_root
        ).astype(jnp.bfloat16),
        "row",
        scatter_dimension=0,
        tiled=True,
    )
    return (grad_logits, head_grad, kl_loss)


def solution(mesh):
    placed = (
        P("row", None),
        P("row", "voc"),
        P("row", "voc"),
        P(),
        P("row"),
        P(None, "voc", None),
        P("voc", None, None, None),
    )
    return jax.shard_map(
        per_device,
        mesh=mesh,
        in_specs=placed,
        out_specs=(P("row", "voc"), P("row", "voc"), P()),
        check_vma=False,
    )
```

profile of v0, /device:TPU:0, one launch (start us, length us, event | category | flops | bytes accessed | tf_op | source)
XLA Modules:
  0.0 265.5 jit_solution(6915176413589126362)
XLA Ops:
  0.6 1.0 copy.49
  1.8 0.2 reduce_window_sum.23
  2.7 2.4 copy.57
  5.2 1.8 copy.59
  6.9 3.1 %gather_fusion = bf16[64,256,128]{2,1,0:T(8,128)(2,1)} fusion(bf16[256,20,128]{2,0,1:T(8,128)(2,1)S(1)} %copy.59, s32[1024]{0:T(1024)S(1)} %pad_clamp_fusion.1), kind=kCustom, calls=%fused_computation | custom fusion | bytes 8388864 | tf_op jit(solution)/shard_map/jit(_take)/gather | solution.py:30
  10.0 4.0 %select_bitcast_fusion = bf16[256,64,128]{2,0,1:T(8,128)(2,1)} fusion(bf16[64,256,128]{2,1,0:T(8,128)(2,1)} %gather_fusion, pred[64]{0:T(512)(128)(4,1)S(1)} %gt.19, pred[64]{0:T(512)(128)(4,1)S(1)} %compare_and_fusion), kind=kLoop, calls=%fused_computation.5 | loop fusion | flops 4194304 | bytes 8388736 | tf_op jit(solution)/shard_map/jit(_where)/select_n | solution.py:28
  14.0 7.4 %all-to-all-start = ((bf16[256,64,128]{2,0,1:T(8,128)(2,1)}), bf16[256,64,128]{2,0,1:T(8,128)(2,1)}, u32[]{:S(2)}, u32[]{:S(2)}) async-start(bf16[256,64,128]{2,0,1:T(8,128)(2,1)} %select_bitcast_fusion), calls=%async_computation | async-start | bytes 8388608 | tf_op jit(solution)/shard_map/all_to_all | solution.py:33
  21.6 0.2 fusion.12
  21.9 0.5 broadcast.277
  22.4 0.7 fusion.25
  23.3 0.5 broadcast.278
  23.8 0.7 fusion.24
  24.8 0.2 select_reduce_fusion.1
  25.3 9.6 %fusion.26 = (f32[256]{0:T(256)S(1)}, f32[256,2048]{1,0:T(8,128)}) fusion(bf16[256,4096]{1,0:T(8,128)(2,1)S(1)} %copy-done, bf16[4096,2048]{1,0:T(8,128)(2,1)} %param.8), kind=kOutput, calls=%fused_computation.61 | convolution fusion | flops 4295491584 | bytes 20972544 | tf_op jit(solution)/shard_map/dot_general | solution.py:62
  34.9 100.9 %pmax.7 = f32[256]{0:T(256)S(1)} all-reduce(f32[256]{0:T(256)S(1)} %get-tuple-element.30), channel_id=1, replica_groups=mesh['row'=1,'voc'=32] {'voc'}, use_global_device_ids=true, to_apply=%region_1.2 | all-reduce | flops 256 | bytes 2048 | tf_op jit(solution)/shard_map/pmax | solution.py:69
  135.8 2.0 exponential_reduce_fusion
  137.8 4.4 %gather_fusion.1 = bf16[32,256,128]{2,1,0:T(8,128)(2,1)} fusion(bf16[256,64,128]{2,0,1:T(8,128)(2,1)} %all-to-all-done, s32[1024]{0:T(1024)S(1)} %pad_clamp_fusion), kind=kCustom, calls=%fused_computation.1 | custom fusion | bytes 4194432 | tf_op jit(solution)/shard_map/jit(_take)/gather | solution.py:38
  142.2 4.0 %fusion.1 = (f32[256]{0:T(256)S(1)}, f32[256,16,128]{0,2,1:T(8,128)}) fusion(f32[256,16,2]{0,2,1:T(2,128)S(1)} %copy.48, bf16[16,2,128,128]{3,2,1,0:T(8,128)(2,1)S(1)} %copy-done.3, bf16[256,16,2,128]{3,0,2,1:T(8,128)(2,1)} %bitcast.52, pred[16,2]{1,0:T(8,128)(4,1)S(1)} %copy.54), kind=kOutput, calls=%fused_computation.6 | convolution fusion | flops 272105216 | bytes 5276704 | tf_op jit(solution)/shard_map/tbkj,bkjc->tbkc/dot_general | solution.py:41
  146.2 2.9 %copy.65 = f32[256,2048]{1,0:T(8,128)} copy(f32[256,2048]{0,1:T(8,128)} %bitcast.53) | data formatting | bytes 4194304 | tf_op jit(solution)/shard_map/reshape | solution.py:51
  149.1 38.1 %all-reduce = (f32[256]{0:T(256)S(1)}, f32[256]{0:T(256)S(1)}) all-reduce(f32[256]{0:T(256)S(1)} %exponential_reduce_fusion, f32[256]{0:T(256)S(1)} %get-tuple-element.18), channel_id=1, replica_groups=mesh['row'=1,'voc'=32] {'voc'}, use_global_device_ids=true, to_apply=%region_3.4 | all-reduce | flops 512 | bytes 4096 | tf_op jit(solution)/shard_map/psum | solution.py:70
  187.2 3.8 %multiply_reduce_fusion = (f32[]{:T(128)}, bf16[256,2048]{1,0:T(8,128)(2,1)S(1)}) fusion(f32[256,2048]{1,0:T(8,128)} %get-tuple-element.31, f32[256]{0:T(256)S(1)} %log_add_fusion, f32[256,2048]{1,0:T(8,128)} %copy.65, f32[256]{0:T(256)S(1)} %get-tuple-element.23), kind=kLoop, calls=%fused_computation.8 | loop fusion | flops 4718591 | bytes 5244932 | tf_op jit(solution)/shard_map/reduce_sum | solution.py:79
  191.0 42.2 %psum.23 = f32[]{:T(128)} all-reduce(f32[]{:T(128)} %get-tuple-element.28), channel_id=1, replica_groups=mesh['row'=1,'voc'=32] {'row','voc'}, use_global_device_ids=true, to_apply=%region_13.14 | all-reduce | flops 1 | bytes 8 | tf_op jit(solution)/shard_map/psum | solution.py:80
  233.3 8.1 %fusion = bf16[4096,2048]{0,1:T(8,128)(2,1)} fusion(bf16[256,2048]{1,0:T(8,128)(2,1)S(1)} %get-tuple-element.29, bf16[256,4096]{1,0:T(8,128)(2,1)S(1)} %copy-done), kind=kOutput, calls=%fused_computation.3 | convolution fusion | flops 4311744512 | bytes 19922944 | tf_op jit(solution)/shard_map/td,tv->dv/dot_general | solution.py:84
  241.3 22.4 %copy.62 = bf16[4096,2048]{1,0:T(8,128)(2,1)} copy(bf16[4096,2048]{0,1:T(8,128)(2,1)} %fusion) | data formatting | bytes 33554432
  (41 shorter events, 1.9 us)
Async XLA Ops:
  0.6 24.6 %copy-start = (bf16[256,4096]{1,0:T(8,128)(2,1)S(1)}, bf16[256,4096]{1,0:T(8,128)(2,1)}, u32[]{:S(2)}) copy-start(bf16[256,4096]{1,0:T(8,128)(2,1)} %param.7) | copy-start | bytes 6291460
  14.0 7.4 %copy-start.2 = (s32[4]{0:T(128)S(1)}, s32[4]{0:T(128)}, u32[]{:S(2)}) copy-start(s32[4]{0:T(128)} %param.11) | copy-start | bytes 52
  14.0 7.6 %copy-start.4 = (f32[4,16,2]{1,2,0:T(2,128)S(1)}, f32[4,16,2]{1,2,0:T(2,128)}, u32[]{:S(2)}) copy-start(f32[4,16,2]{1,2,0:T(2,128)} %param.12) | copy-start | bytes 1540
  14.0 123.8 %all-to-all-start = ((bf16[256,64,128]{2,0,1:T(8,128)(2,1)}), bf16[256,64,128]{2,0,1:T(8,128)(2,1)}, u32[]{:S(2)}, u32[]{:S(2)}) async-start(bf16[256,64,128]{2,0,1:T(8,128)(2,1)} %select_bitcast_fusion), calls=%async_computation | async-start | bytes 8388608 | tf_op jit(solution)/shard_map/all_to_all | solution.py:33
  137.8 4.4 %copy-start.3 = (bf16[16,2,128,128]{3,2,1,0:T(8,128)(2,1)S(1)}, bf16[16,2,128,128]{3,2,1,0:T(8,128)(2,1)}, u32[]{:S(2)}) copy-start(bf16[16,2,128,128]{3,2,1,0:T(8,128)(2,1)} %param.13) | copy-start | bytes 3145732
  191.0 50.3 %copy-start.1 = (bf16[256,2048]{1,0:T(8,128)(2,1)}, bf16[256,2048]{1,0:T(8,128)(2,1)S(1)}, u32[]{:S(2)}) copy-start(bf16[256,2048]{1,0:T(8,128)(2,1)S(1)} %get-tuple-element.29) | copy-start | bytes 3145732
where the time goes:
time: 267 us; the launch traced here: 266 us
  blocking collectives  181 us (68%)
  local copies, waits for them, and re-layouts  40.5 us (15%)
  matrix products  21.9 us (8%)
  other arithmetic  12 us (4%)
  starting transfers between devices  7.43 us (3%)
    pmax x1, blocking collectives, per_device(): peak = lax.pmax(jnp.max(logits, axis=1), 'voc')  101 us
    psum x1, blocking collectives, per_device(): kl_loss = lax.psum(kl_partial, ('row', 'voc')) / rows_total  42.2 us
    psum x1, blocking collectives, per_device(): lax.psum((jnp.sum(jnp.exp(logits - peak[:, None]), axis=1), local_total),...  38.1 us
    unnamed x13, local copies, waits for them, and re-layouts  25.9 us
    dot_general x1, matrix products, per_device(): jnp.dot(columns, lax.all_gather(student_head, 'row', axis=0, tiled=True),...  9.62 us
    dot_general x1, matrix products, per_device(): jnp.einsum('td,tv->dv', columns, grad_logits, preferred_element_type=jnp....  8.08 us
    all_to_all x1, starting transfers between devices, map_teacher(): lax.all_to_all(outgoing, 'voc', split_axis=1, concat_axis=1, tiled=True)  7.43 us
  transfers between devices with their start and end apart: 1, of which 0 were waited for; matrix products, arithmetic and copies ran while one was open for 6% of the time, Pallas kernels for 0%

commit v1 on v0

v1 whole, which is shorter than its diff:
```python
import functools
import math

import jax
import jax.numpy as jnp
from jax import lax
from jax.experimental import pallas as pl
from jax.experimental.pallas import tpu as pltpu
from jax.sharding import PartitionSpec as P

MESH = pl.DeviceIdType.MESH
STEPS = 8


def route_tables(block_map, per_shard, voc_count, own_index):
    entries = block_map.size // voc_count
    wanted = block_map.reshape(voc_count, entries)
    sources = wanted // per_shard
    place = jnp.arange(entries, dtype=jnp.int32)
    big = entries * per_shard
    key = place[None, :] * per_shard + (wanted - sources * per_shard)
    owned = sources == own_index
    first = jnp.min(jnp.where(owned, key, big), axis=1)
    last = jnp.max(jnp.where(owned, key, -1), axis=1)
    take_first = first % per_shard
    take_second = jnp.where(last > first, last % per_shard, per_shard)
    mine = lax.dynamic_index_in_dim(sources, own_index, 0, keepdims=False)
    earlier = jnp.max(
        jnp.where((mine[None, :] == mine[:, None]) & (place[None, :] < place[:, None]), 1, 0), axis=1
    )
    slot_of = jnp.where(earlier > 0, voc_count, mine)
    slots = jnp.arange(voc_count + 1, dtype=jnp.int32)
    entry_of = jnp.max(jnp.where(slot_of[None, :] == slots[:, None], place[None, :], 0), axis=1)
    return take_first, take_second, slot_of, entry_of


def exchange_kernel(
    n,
    take_first,
    take_second,
    slot_of,
    entry_of,
    context_ref,
    gates_ref,
    hidden_ref,
    head_ref,
    teacher_ref,
    tiles_ref,
    logits_ref,
    mapped_ref,
    turned_ref,
    cols_ref,
    kl_ref,
    shelf,
    outgoing,
    incoming,
    extra,
    landing,
    products,
    stats_out,
    stats_in,
    send_sem,
    recv_sem,
    extra_send,
    extra_recv,
    stat_send,
    stat_recv,
):
    step = pl.program_id(0)
    me = lax.axis_index("voc")
    levels = n.bit_length() - 1
    bits = [(me // 2**b) % 2 for b in range(levels)]
    tokens, width = hidden_ref.shape
    block = tiles_ref.shape[-1]
    fanout = slot_of.shape[0] * block // mapped_ref.shape[1]
    chunk = head_ref.shape[1]
    windows = context_ref.shape[0]
    entries = slot_of.shape[0]

    def partner(d):
        return sum(((bits[b] + (d >> b)) % 2) * 2**b for b in range(levels))

    def reverse(e):
        return sum(((e // 2**b) % 2) * 2 ** (levels - 1 - b) for b in range(levels))

    order = sorted(range(1, n), reverse=True)

    def main_copy(d):
        return pltpu.make_async_remote_copy(
            src_ref=outgoing.at[partner(d)],
            dst_ref=incoming.at[me],
            send_sem=send_sem.at[d],
            recv_sem=recv_sem.at[d],
            device_id={"voc": partner(d)},
            device_id_type=MESH,
        )

    def main_recv(d):
        return pltpu.make_async_remote_copy(
            src_ref=outgoing.at[partner(d)],
            dst_ref=incoming.at[partner(d)],
            send_sem=send_sem.at[d],
            recv_sem=recv_sem.at[d],
            device_id={"voc": partner(d)},
            device_id_type=MESH,
        )

    def region(s):
        return sum(bits[b] * (n >> (b + 1)) for b in range(s))

    def extra_copy(s):
        half = n >> (s + 1)
        away = region(s) + (1 - bits[s]) * half
        return pltpu.make_async_remote_copy(
            src_ref=extra.at[pl.ds(away, half)],
            dst_ref=landing.at[pl.ds(n - 2 * half, half)],
            send_sem=extra_send.at[s],
            recv_sem=extra_recv.at[s],
            device_id={"voc": partner(1 << s)},
            device_id_type=MESH,
        )

    def extra_add(s):
        half = n >> (s + 1)
        kept = region(s) + bits[s] * half

        def add(i, carry):
            extra[kept + i] = extra[kept + i] + landing[n - 2 * half + i]
            return carry

        lax.fori_loop(0, half, add, 0)

    def stat_copy(d, owner):
        return pltpu.make_async_remote_copy(
            src_ref=stats_out,
            dst_ref=stats_in.at[owner],
            send_sem=stat_send.at[d],
            recv_sem=stat_recv.at[d],
            device_id={"voc": partner(d)},
            device_id_type=MESH,
        )

    @pl.when(step == 0)
    def _():
        barrier = pltpu.get_barrier_semaphore()
        for d in range(1, n):
            pl.semaphore_signal(barrier, inc=1, device_id={"voc": partner(d)}, device_id_type=MESH)

        def fill(e, carry):
            extra[reverse(e)] = shelf[take_second[e]]
            outgoing[e] = shelf[take_first[e]]
            return carry

        for i in range(shelf.shape[0] - 1):
            shelf[i] = teacher_ref[:, i * block : (i + 1) * block]
        shelf[shelf.shape[0] - 1] = jnp.zeros(shelf.shape[1:], shelf.dtype)

        lax.fori_loop(0, n, fill, 0)
        incoming[me] = outgoing[me]
        pl.semaphore_wait(barrier, n - 1)
        extra_copy(0).start()
        for d in order:
            main_copy(d).start()

    logits_ref[:, pl.ds(pl.multiple_of(step * chunk, chunk), chunk)] = jnp.dot(
        hidden_ref[...], head_ref[...], preferred_element_type=jnp.float32
    )
    rows = turned_ref.shape[0]
    turned_ref[...] = hidden_ref[:, pl.ds(pl.multiple_of(step * rows, rows), rows)].T

    for s in range(levels):

        @pl.when(step == s + 1)
        def _(s=s):
            extra_copy(s).wait()
            extra_add(s)
            if s + 1 < levels:
                extra_copy(s + 1).start()
            else:
                incoming[n] = extra[region(levels)]

    def multiply(slot):
        entry = entry_of[slot]
        value = jnp.dot(incoming[slot], tiles_ref[entry], preferred_element_type=jnp.float32)
        span = tokens // windows
        for w in range(windows):
            gate = gates_ref[context_ref[w] * entries + entry]
            products[slot, w * span : (w + 1) * span] = value[w * span : (w + 1) * span] * gate

    @pl.when(step == STEPS - 1)
    def _():
        peak = jnp.max(logits_ref[...], axis=1, keepdims=True)
        summed = jnp.sum(jnp.exp(logits_ref[...] - peak), axis=1, keepdims=True)
        multiply(me)
        multiply(n)
        for d in order:
            main_recv(d).wait_recv()
            multiply(partner(d))
        total = jnp.zeros((tokens, block), jnp.float32)
        cross = jnp.zeros((tokens, block), jnp.float32)
        for b in range(entries // fanout):
            value = products[slot_of[b * fanout]]
            for k in range(1, fanout):
                value = value + products[slot_of[b * fanout + k]]
            mapped_ref[:, b * block : (b + 1) * block] = value
            total = total + value
            cross = cross + value * (
                jnp.log(value) - (logits_ref[:, b * block : (b + 1) * block] - peak)
            )
        total = jnp.sum(total, axis=1, keepdims=True)
        cross = jnp.sum(cross, axis=1, keepdims=True)
        lane = lax.broadcasted_iota(jnp.int32, (tokens, block), 1)
        packed = jnp.where(
            lane == 0, peak, jnp.where(lane == 1, summed, jnp.where(lane == 2, total, cross))
        )
        stats_out[...] = packed.T[:8]
        stats_in[me] = stats_out[...]
        for d in order:
            stat_copy(d, me).start()
        for d in order:
            stat_copy(d, partner(d)).wait_recv()
        peaks = stats_in[:, 0, :]
        sums = stats_in[:, 1, :]
        totals = stats_in[:, 2, :]
        crosses = stats_in[:, 3, :]
        top = jnp.max(peaks, axis=0, keepdims=True)
        log_norm = top + jnp.log(jnp.sum(sums * jnp.exp(peaks - top), axis=0, keepdims=True))
        row_total = jnp.sum(totals, axis=0, keepdims=True)
        weighted = jnp.sum(crosses + totals * (log_norm - peaks), axis=0, keepdims=True)
        divergence = weighted / row_total - jnp.log(row_total)
        kl_ref[...] = jnp.broadcast_to(jnp.sum(divergence, axis=1, keepdims=True), kl_ref.shape)
        line = lax.broadcasted_iota(jnp.int32, (block, tokens), 0)
        cols_ref[...] = jnp.where(line == 0, log_norm, 1.0 / row_total).T
        for d in order:
            main_copy(d).wait_send()
            stat_copy(d, me).wait_send()


def exchange(hidden, head, teacher, tables, context, gates, tiles):
    n = lax.axis_size("voc")
    tokens, width = hidden.shape
    cols = head.shape[1]
    block = tiles.shape[-1]
    levels = n.bit_length() - 1
    smem = pl.BlockSpec(memory_space=pltpu.SMEM)

    def whole(shape):
        return pl.BlockSpec(shape, lambda i: (0,) * len(shape), pipeline_mode=pl.Buffered(1))

    return pl.pallas_call(
        functools.partial(exchange_kernel, n),
        grid=(STEPS,),
        out_shape=(
            jax.ShapeDtypeStruct((tokens, cols), jnp.float32),
            jax.ShapeDtypeStruct((tokens, cols), jnp.float32),
            jax.ShapeDtypeStruct((width, tokens), hidden.dtype),
            jax.ShapeDtypeStruct((tokens, block), jnp.float32),
            jax.ShapeDtypeStruct((8, 128), jnp.float32),
        ),
        in_specs=[smem] * 6
        + [
            whole((tokens, width)),
            pl.BlockSpec((width, cols // STEPS), lambda i: (0, i)),
            whole(teacher.shape),
            whole(tiles.shape),
        ],
        out_specs=(
            whole((tokens, cols)),
            whole((tokens, cols)),
            pl.BlockSpec((width // STEPS, tokens), lambda i: (i, 0)),
            whole((tokens, block)),
            whole((8, 128)),
        ),
        scratch_shapes=[
            pltpu.VMEM((teacher.shape[1] // block + 1, tokens, block), teacher.dtype),
            pltpu.VMEM((n, tokens, block), teacher.dtype),
            pltpu.VMEM((n + 1, tokens, block), teacher.dtype),
            pltpu.VMEM((n, tokens, block), teacher.dtype),
            pltpu.VMEM((n, tokens, block), teacher.dtype),
            pltpu.VMEM((n + 1, tokens, block), jnp.float32),
            pltpu.VMEM((8, tokens), jnp.float32),
            pltpu.VMEM((n, 8, tokens), jnp.float32),
            pltpu.SemaphoreType.DMA((n,)),
            pltpu.SemaphoreType.DMA((n,)),
            pltpu.SemaphoreType.DMA((levels,)),
            pltpu.SemaphoreType.DMA((levels,)),
            pltpu.SemaphoreType.DMA((n,)),
            pltpu.SemaphoreType.DMA((n,)),
        ],
        compiler_params=pltpu.CompilerParams(
            collective_id=0, has_side_effects=True, vmem_limit_bytes=48 << 20
        ),
        name="exchange",
    )(*tables, context, gates, hidden, head, teacher, tiles)


def gradient_kernel(vocab, inv_root, cols_ref, logits_ref, mapped_ref, turned_ref, grad_ref, out_ref):
    log_norm = cols_ref[:, 0:1]
    inverse = cols_ref[:, 1:2]
    grad = (
        vocab * (jnp.exp(logits_ref[...] - log_norm) - mapped_ref[...] * inverse)
    ).astype(grad_ref.dtype)
    grad_ref[...] = grad
    out_ref[...] = (
        jnp.dot(turned_ref[...], grad, preferred_element_type=jnp.float32) * inv_root
    ).astype(out_ref.dtype)


def gradients(logits, mapped, turned, cols, vocab, inv_root):
    tokens, columns = logits.shape
    width = turned.shape[0]
    chunk = columns // STEPS
    part = pl.BlockSpec((tokens, chunk), lambda i: (0, i))
    return pl.pallas_call(
        functools.partial(gradient_kernel, float(vocab), inv_root),
        grid=(STEPS,),
        out_shape=(
            jax.ShapeDtypeStruct((tokens, columns), jnp.bfloat16),
            jax.ShapeDtypeStruct((width, columns), jnp.bfloat16),
        ),
        in_specs=[
            pl.BlockSpec(cols.shape, lambda i: (0, 0), pipeline_mode=pl.Buffered(1)),
            part,
            part,
            pl.BlockSpec(turned.shape, lambda i: (0, 0), pipeline_mode=pl.Buffered(1)),
        ],
        out_specs=(part, pl.BlockSpec((width, chunk), lambda i: (0, i))),
        compiler_params=pltpu.CompilerParams(vmem_limit_bytes=32 << 20),
        name="gradients",
    )(cols, logits, mapped, turned)


def per_device(
    hidden_states, student_head, teacher_probs, block_map, context, map_gates, map_tiles
):
    voc_count = lax.axis_size("voc")
    own_index = lax.axis_index("voc")
    rows_total = hidden_states.shape[0] * lax.axis_size("row")
    inv_root = 1.0 / math.sqrt(rows_total)
    vocab_total = student_head.shape[1] * voc_count
    blocks, fanout, block, _ = map_tiles.shape
    head = lax.all_gather(student_head, "row", axis=0, tiled=True)
    tables = route_tables(block_map, teacher_probs.shape[1] // block, voc_count, own_index)
    logits, mapped, turned, cols, kl = exchange(
        hidden_states,
        head,
        teacher_probs,
        tables,
        context,
        map_gates.reshape(-1),
        map_tiles.reshape(blocks * fanout, block, block),
    )
    grad_logits, head_part = gradients(logits, mapped, turned, cols, vocab_total, inv_root)
    kl_loss = lax.psum(kl[0, 0], "row") / rows_total
    head_grad = lax.psum_scatter(head_part, "row", scatter_dimension=0, tiled=True)
    return (grad_logits, head_grad, kl_loss)


def solution(mesh):
    placed = (
        P("row", None),
        P("row", "voc"),
        P("row", "voc"),
        P(),
        P("row"),
        P(None, "voc", None),
        P("voc", None, None, None),
    )
    return jax.shard_map(
        per_device,
        mesh=mesh,
        in_specs=placed,
        out_specs=(P("row", "voc"), P("row", "voc"), P()),
        check_vma=False,
    )
```

time: 267 us -> 107 us (0.40)
  blocking collectives: 181 us -> 0 us
  Pallas kernels: 0 us -> 94.4 us
  local copies, waits for them, and re-layouts: 40.5 us -> 8.72 us
  matrix products: 21.9 us -> 0 us
  other arithmetic: 12 us -> 1.29 us
  starting transfers between devices: 7.43 us -> 0 us
    pmax x1 -> x0, blocking collectives: 101 us -> none  [per_device(): peak = lax.pmax(jnp.max(logits, axis=1), 'voc')]
    pallas_call x0 -> x2, Pallas kernels: none -> 94.4 us  [the longest x1 84.7 us: exchange(): pl.pallas_call(functools.partial(exchange_kernel, n), grid=(STEPS,), out_...]
    psum x2 -> x0, blocking collectives: 80.3 us -> none  [the longest x1 42.2 us: per_device(): kl_loss = lax.psum(kl_partial, ('row', 'voc')) / rows_total]
    dot_general x4 -> x0, matrix products: 21.9 us -> none  [the longest x1 9.62 us: per_device(): jnp.dot(columns, lax.all_gather(student_head, 'row', axis=0, tiled=True),...]
    unnamed x13 -> x11, local copies, waits for them, and re-layouts: 25.9 us -> 7.15 us
    gather x2 -> x0, local copies, waits for them, and re-layouts: 7.51 us -> none  [the longest x1 4.41 us: map_teacher(): jnp.take(incoming, sources * capacity + position, axis=1)]
    all_to_all x1 -> x0, starting transfers between devices: 7.43 us -> none  [map_teacher(): lax.all_to_all(outgoing, 'voc', split_axis=1, concat_axis=1, tiled=True)]
    reduce_sum x4 -> x0, other arithmetic: 6.17 us -> none  [the longest x1 3.82 us: per_device(): jnp.sum(target * (jnp.log(target) - logits + log_norm[:, None]))]
  transfers between devices with their start and end apart: 1 -> 0, of which waited for: 0 -> 0; matrix products, arithmetic and copies ran while one was open for 6% -> 0% of each run, Pallas kernels for 0% -> 0%
where the time goes in v1:
time: 107 us
  Pallas kernels  94.4 us (88%)
  local copies, waits for them, and re-layouts  8.72 us (8%)
  between operations  2.51 us (2%)
  other arithmetic  1.29 us (1%)
    pallas_call x1, Pallas kernels, exchange(): pl.pallas_call(functools.partial(exchange_kernel, n), grid=(STEPS,), out_...  84.7 us
    pallas_call x1, Pallas kernels, gradients(): pl.pallas_call(functools.partial(gradient_kernel, float(vocab), inv_root)...  9.71 us
    unnamed x11, local copies, waits for them, and re-layouts  7.15 us

profile of v1, /device:TPU:0, one launch (start us, length us, event | category | flops | bytes accessed | tf_op | source)
XLA Modules:
  0.0 106.9 jit_solution(11914427297685560639)
XLA Ops:
  0.7 0.1 add.33
  0.7 0.7 subtract_add_fusion
  1.5 0.1 reduce_max.35
  1.6 0.1 reduce_max.36
  1.7 0.1 reduce_min.14
  1.8 0.1 reduce_min.18
  1.9 0.8 copy.18
  2.7 0.1 reshape.49.gates_ref
  2.8 0.2 copy.16
  3.0 0.2 and.23
  3.2 0.1 copy.17
  3.3 0.2 div.17
  3.5 0.2 select_reduce_fusion.1
  3.7 0.1 select_reduce_fusion.entry_of
  3.8 0.0 copy-start.2
  3.8 1.3 %copy-done.2 = bf16[256,2560]{1,0:T(8,128)(2,1)S(1)} copy-done((bf16[256,2560]{1,0:T(8,128)(2,1)S(1)}, bf16[256,2560]{1,0:T(8,128)(2,1)}, u32[]{:S(2)}) %copy-start.2) | copy-done | bytes 1310744
  5.2 1.2 %copy-done.3 = bf16[16,2,128,128]{3,2,1,0:T(8,128)(2,1)S(1)} copy-done((bf16[16,2,128,128]{3,2,1,0:T(8,128)(2,1)S(1)}, bf16[16,2,128,128]{3,2,1,0:T(8,128)(2,1)}, u32[]{:S(2)}) %copy-start.3) | copy-done | bytes 1048600
  6.4 0.7 copy-done.4
  7.0 84.7 %exchange.1 = (f32[256,2048]{1,0:T(8,128)S(1)}, f32[256,2048]{1,0:T(8,128)}, bf16[4096,256]{1,0:T(8,128)(2,1)}, f32[256,128]{1,0:T(8,128)S(1)}, f32[8,128]{1,0:T(8,128)S(1)}) custom-call(s32[32]{0:T(128)S(1)} %get-tuple-element.23.take_first, s32[32]{0:T(128)S(1)} %get-tuple-element.22.take_second, s32[32]{0:T(128)S(1)} %get-tuple-element.24.slot_of, ...), custom_call_target="tpu_custom_call" | custom-call | tf_op jit(solution)/shard_map/exchange/pallas_call | solution.py:250
  91.8 0.5 slice.3
  92.9 0.0 copy-start
  92.9 1.6 %copy-done = f32[256,2048]{1,0:T(8,128)S(1)} copy-done((f32[256,2048]{1,0:T(8,128)S(1)}, f32[256,2048]{1,0:T(8,128)}, u32[]{:S(2)}) %copy-start) | copy-done | bytes 2097176
  94.5 1.6 %copy-done.1 = bf16[4096,256]{1,0:T(8,128)(2,1)S(1)} copy-done((bf16[4096,256]{1,0:T(8,128)(2,1)S(1)}, bf16[4096,256]{1,0:T(8,128)(2,1)}, u32[]{:S(2)}) %copy-start.1) | copy-done | bytes 2097176
  96.1 9.7 %gradients.1 = (bf16[256,2048]{1,0:T(8,128)(2,1)}, bf16[4096,2048]{1,0:T(8,128)(2,1)}) custom-call(f32[256,128]{1,0:T(8,128)S(1)} %get-tuple-element.10.cols_ref, f32[256,2048]{1,0:T(8,128)S(1)} %get-tuple-element.11.logits_ref, f32[256,2048]{1,0:T(8,128)S(1)} %copy-done, bf16[4096,256]{1,0:T(8,128)(2,1)S(1)} %copy-done.1), custom_call_target="tpu_custom_call" | custom-call | tf_op jit(solution)/shard_map/gradients/pallas_call | solution.py:314
  (9 shorter events, 0.1 us)
Async XLA Ops:
  3.8 1.3 %copy-start.2 = (bf16[256,2560]{1,0:T(8,128)(2,1)S(1)}, bf16[256,2560]{1,0:T(8,128)(2,1)}, u32[]{:S(2)}) copy-start(bf16[256,2560]{1,0:T(8,128)(2,1)} %teacher_ref.1) | copy-start | bytes 3932164
  5.1 1.2 %copy-start.3 = (bf16[16,2,128,128]{3,2,1,0:T(8,128)(2,1)S(1)}, bf16[16,2,128,128]{3,2,1,0:T(8,128)(2,1)}, u32[]{:S(2)}) copy-start(bf16[16,2,128,128]{3,2,1,0:T(8,128)(2,1)} %param.13) | copy-start | bytes 3145732
  6.4 0.7 copy-start.4
  92.9 1.6 %copy-start = (f32[256,2048]{1,0:T(8,128)S(1)}, f32[256,2048]{1,0:T(8,128)}, u32[]{:S(2)}) copy-start(f32[256,2048]{1,0:T(8,128)} %get-tuple-element.12.mapped_ref) | copy-start | bytes 6291460
  94.5 1.6 %copy-start.1 = (bf16[4096,256]{1,0:T(8,128)(2,1)S(1)}, bf16[4096,256]{1,0:T(8,128)(2,1)}, u32[]{:S(2)}) copy-start(bf16[4096,256]{1,0:T(8,128)(2,1)} %get-tuple-element.13.turned_ref) | copy-start | bytes 6291460

commit v2 on v1

--- a/solution.py
+++ b/solution.py
@@ -42,15 +42,19 @@
     entry_of,
     context_ref,
     gates_ref,
-    hidden_ref,
+    hidden_hbm,
     head_ref,
     teacher_ref,
+    tiles_hbm,
+    logits_hbm,
+    mapped_hbm,
+    turned_ref,
+    cols_ref,
+    hidden_ref,
     tiles_ref,
     logits_ref,
     mapped_ref,
-    turned_ref,
-    cols_ref,
-    kl_ref,
+    local_sem,
     shelf,
     outgoing,
     incoming,
@@ -83,7 +87,16 @@
     def reverse(e):
         return sum(((e // 2**b) % 2) * 2 ** (levels - 1 - b) for b in range(levels))
 
-    order = sorted(range(1, n), reverse=True)
+    half_count = n // 2
+    order = [
+        d for d in reversed(range(1, n))
+    ]
+    batch = -(-len(order) // levels)
+    late = {s: min(batch * (3 * s - 8), n - 2) for s in range(3, levels)}
+    load_hidden = pltpu.make_async_copy(hidden_hbm, hidden_ref, local_sem.at[0])
+    load_tiles = pltpu.make_async_copy(tiles_hbm, tiles_ref, local_sem.at[1])
+    save_logits = pltpu.make_async_copy(logits_ref, logits_hbm, local_sem.at[2])
+    save_mapped = pltpu.make_async_copy(mapped_ref, mapped_hbm, local_sem.at[3])
 
     def main_copy(d):
         return pltpu.make_async_remote_copy(
@@ -140,8 +153,22 @@
             device_id_type=MESH,
         )
 
+    def send_batch(s):
+        for d in order[s * batch : (s + 1) * batch]:
+            main_copy(d).start()
+
+    def extra_finish(s):
+        extra_copy(s).wait()
+        extra_add(s)
+        if s + 1 < levels:
+            extra_copy(s + 1).start()
+            send_batch(s + 1)
+        else:
+            incoming[n] = extra[region(levels)]
+
     @pl.when(step == 0)
     def _():
+        load_hidden.start()
         barrier = pltpu.get_barrier_semaphore()
         for d in range(1, n):
             pl.semaphore_signal(barrier, inc=1, device_id={"voc": partner(d)}, device_id_type=MESH)
@@ -159,8 +186,9 @@
         incoming[me] = outgoing[me]
         pl.semaphore_wait(barrier, n - 1)
         extra_copy(0).start()
-        for d in order:
-            main_copy(d).start()
+        send_batch(0)
+        load_tiles.start()
+        load_hidden.wait()
 
     logits_ref[:, pl.ds(pl.multiple_of(step * chunk, chunk), chunk)] = jnp.dot(
         hidden_ref[...], head_ref[...], preferred_element_type=jnp.float32
@@ -168,16 +196,11 @@
     rows = turned_ref.shape[0]
     turned_ref[...] = hidden_ref[:, pl.ds(pl.multiple_of(step * rows, rows), rows)].T
 
-    for s in range(levels):
-
-        @pl.when(step == s + 1)
+    for s in range(min(levels, 3)):
+
+        @pl.when(step == (1, 3, 6)[s])
         def _(s=s):
-            extra_copy(s).wait()
-            extra_add(s)
-            if s + 1 < levels:
-                extra_copy(s + 1).start()
-            else:
-                incoming[n] = extra[region(levels)]
+            extra_finish(s)
 
     def multiply(slot):
         entry = entry_of[slot]
@@ -189,13 +212,18 @@
 
     @pl.when(step == STEPS - 1)
     def _():
+        save_logits.start()
+        load_tiles.wait()
         peak = jnp.max(logits_ref[...], axis=1, keepdims=True)
         summed = jnp.sum(jnp.exp(logits_ref[...] - peak), axis=1, keepdims=True)
         multiply(me)
-        multiply(n)
-        for d in order:
+        for i, d in enumerate(order):
             main_recv(d).wait_recv()
             multiply(partner(d))
+            for s in late:
+                if late[s] == i:
+                    extra_finish(s)
+        multiply(n)
         total = jnp.zeros((tokens, block), jnp.float32)
         cross = jnp.zeros((tokens, block), jnp.float32)
         for b in range(entries // fanout):
@@ -207,6 +235,7 @@
             cross = cross + value * (
                 jnp.log(value) - (logits_ref[:, b * block : (b + 1) * block] - peak)
             )
+        save_mapped.start()
         total = jnp.sum(total, axis=1, keepdims=True)
         cross = jnp.sum(cross, axis=1, keepdims=True)
         lane = lax.broadcasted_iota(jnp.int32, (tokens, block), 1)
@@ -228,12 +257,16 @@
         row_total = jnp.sum(totals, axis=0, keepdims=True)
         weighted = jnp.sum(crosses + totals * (log_norm - peaks), axis=0, keepdims=True)
         divergence = weighted / row_total - jnp.log(row_total)
-        kl_ref[...] = jnp.broadcast_to(jnp.sum(divergence, axis=1, keepdims=True), kl_ref.shape)
+        divergence = jnp.sum(divergence, axis=1, keepdims=True)
         line = lax.broadcasted_iota(jnp.int32, (block, tokens), 0)
-        cols_ref[...] = jnp.where(line == 0, log_norm, 1.0 / row_total).T
+        cols_ref[...] = jnp.where(
+            line == 0, log_norm, jnp.where(line == 1, 1.0 / row_total, divergence)
+        ).T
         for d in order:
             main_copy(d).wait_send()
             stat_copy(d, me).wait_send()
+        save_logits.wait()
+        save_mapped.wait()
 
 
 def exchange(hidden, head, teacher, tables, context, gates, tiles):
@@ -242,6 +275,7 @@
     cols = head.shape[1]
     block = tiles.shape[-1]
     levels = n.bit_length() - 1
+    hbm = pl.BlockSpec(memory_space=pl.ANY)
     smem = pl.BlockSpec(memory_space=pltpu.SMEM)
 
     def whole(shape):
@@ -255,23 +289,26 @@
             jax.ShapeDtypeStruct((tokens, cols), jnp.float32),
             jax.ShapeDtypeStruct((width, tokens), hidden.dtype),
             jax.ShapeDtypeStruct((tokens, block), jnp.float32),
-            jax.ShapeDtypeStruct((8, 128), jnp.float32),
         ),
         in_specs=[smem] * 6
         + [
-            whole((tokens, width)),
+            hbm,
             pl.BlockSpec((width, cols // STEPS), lambda i: (0, i)),
             whole(teacher.shape),
-            whole(tiles.shape),
+            hbm,
         ],
         out_specs=(
-            whole((tokens, cols)),
-            whole((tokens, cols)),
+            hbm,
+            hbm,
             pl.BlockSpec((width // STEPS, tokens), lambda i: (i, 0)),
             whole((tokens, block)),
-            whole((8, 128)),
         ),
         scratch_shapes=[
+            pltpu.VMEM((tokens, width), hidden.dtype),
+            pltpu.VMEM(tiles.shape, tiles.dtype),
+            pltpu.VMEM((tokens, cols), jnp.float32),
+            pltpu.VMEM((tokens, cols), jnp.float32),
+            pltpu.SemaphoreType.DMA((4,)),
             pltpu.VMEM((teacher.shape[1] // block + 1, tokens, block), teacher.dtype),
             pltpu.VMEM((n, tokens, block), teacher.dtype),
             pltpu.VMEM((n + 1, tokens, block), teacher.dtype),
@@ -288,13 +325,19 @@
             pltpu.SemaphoreType.DMA((n,)),
         ],
         compiler_params=pltpu.CompilerParams(
-            collective_id=0, has_side_effects=True, vmem_limit_bytes=48 << 20
+            collective_id=0, has_side_effects=True, vmem_limit_bytes=60 << 20
         ),
         name="exchange",
     )(*tables, context, gates, hidden, head, teacher, tiles)
 
 
-def gradient_kernel(vocab, inv_root, cols_ref, logits_ref, mapped_ref, turned_ref, grad_ref, out_ref):
+def gradient_kernel(
+    vocab, inv_root, rows, cols_ref, logits_ref, mapped_ref, turned_ref, grad_ref, out_ref, kl_ref
+):
+    @pl.when(pl.program_id(0) == 0)
+    def _():
+        kl_ref[0, 0] = cols_ref[0, 2] * (1.0 / rows)
+
     log_norm = cols_ref[:, 0:1]
     inverse = cols_ref[:, 1:2]
     grad = (
@@ -306,17 +349,18 @@
     ).astype(out_ref.dtype)
 
 
-def gradients(logits, mapped, turned, cols, vocab, inv_root):
+def gradients(logits, mapped, turned, cols, vocab, inv_root, rows):
     tokens, columns = logits.shape
     width = turned.shape[0]
     chunk = columns // STEPS
     part = pl.BlockSpec((tokens, chunk), lambda i: (0, i))
     return pl.pallas_call(
-        functools.partial(gradient_kernel, float(vocab), inv_root),
+        functools.partial(gradient_kernel, float(vocab), inv_root, rows),
         grid=(STEPS,),
         out_shape=(
             jax.ShapeDtypeStruct((tokens, columns), jnp.bfloat16),
             jax.ShapeDtypeStruct((width, columns), jnp.bfloat16),
+            jax.ShapeDtypeStruct((1, 1), jnp.float32),
         ),
         in_specs=[
             pl.BlockSpec(cols.shape, lambda i: (0, 0), pipeline_mode=pl.Buffered(1)),
@@ -324,8 +368,12 @@
             part,
             pl.BlockSpec(turned.shape, lambda i: (0, 0), pipeline_mode=pl.Buffered(1)),
         ],
-        out_specs=(part, pl.BlockSpec((width, chunk), lambda i: (0, i))),
-        compiler_params=pltpu.CompilerParams(vmem_limit_bytes=32 << 20),
+        out_specs=(
+            part,
+            pl.BlockSpec((width, chunk), lambda i: (0, i)),
+            pl.BlockSpec(memory_space=pltpu.SMEM),
+        ),
+        compiler_params=pltpu.CompilerParams(vmem_limit_bytes=60 << 20),
         name="gradients",
     )(cols, logits, mapped, turned)
 
@@ -341,7 +389,7 @@
     blocks, fanout, block, _ = map_tiles.shape
     head = lax.all_gather(student_head, "row", axis=0, tiled=True)
     tables = route_tables(block_map, teacher_probs.shape[1] // block, voc_count, own_index)
-    logits, mapped, turned, cols, kl = exchange(
+    logits, mapped, turned, cols = exchange(
         hidden_states,
         head,
         teacher_probs,
@@ -350,8 +398,10 @@
         map_gates.reshape(-1),
         map_tiles.reshape(blocks * fanout, block, block),
     )
-    grad_logits, head_part = gradients(logits, mapped, turned, cols, vocab_total, inv_root)
-    kl_loss = lax.psum(kl[0, 0], "row") / rows_total
+    grad_logits, head_part, kl = gradients(
+        logits, mapped, turned, cols, vocab_total, inv_root, rows_total
+    )
+    kl_loss = lax.psum(kl.reshape(()), "row")
     head_grad = lax.psum_scatter(head_part, "row", scatter_dimension=0, tiled=True)
     return (grad_logits, head_grad, kl_loss)
 

time: 107 us -> 94.2 us (0.88)
  local copies, waits for them, and re-layouts: 8.72 us -> 2.35 us
  Pallas kernels: 94.4 us -> 88.4 us
  between operations: 2.51 us -> 0.7 us
    pallas_call x1, Pallas kernels: 84.7 us -> 76.2 us  [exchange(): pl.pallas_call(functools.partial(exchange_kernel, n), grid=(STEPS,), out_...]
    unnamed x11 -> x1, local copies, waits for them, and re-layouts: 7.15 us -> 0.78 us
    pallas_call x1, Pallas kernels: 9.71 us -> 12.3 us  [gradients(): pl.pallas_call(functools.partial(gradient_kernel, float(vocab), inv_root,...]
where the time goes in v2:
time: 94.2 us; the launch traced here: 93.8 us
  Pallas kernels  88.4 us (94%)
  local copies, waits for them, and re-layouts  2.35 us (2%)
  other arithmetic  2.29 us (2%)
    pallas_call x1, Pallas kernels, exchange(): pl.pallas_call(functools.partial(exchange_kernel, n), grid=(STEPS,), out_...  76.2 us
    pallas_call x1, Pallas kernels, gradients(): pl.pallas_call(functools.partial(gradient_kernel, float(vocab), inv_root,...  12.3 us

profile of v2, /device:TPU:0, one launch (start us, length us, event | category | flops | bytes accessed | tf_op | source)
XLA Modules:
  0.0 93.8 jit_solution(9600581056067871288)
XLA Ops:
  0.7 0.1 add.33
  0.7 0.7 subtract_add_fusion
  1.5 0.1 reduce_max.35
  1.6 0.1 reduce_max.36
  1.7 0.1 reduce_min.14
  1.8 0.1 reduce_min.18
  1.9 0.8 copy.18
  2.7 0.7 reshape.50.gates_ref
  3.3 0.2 copy.16
  3.5 0.2 and.23
  3.7 0.1 copy.17
  3.9 0.2 div.12
  4.0 0.2 select_reduce_fusion.1
  4.2 0.5 compare_select_fusion
  4.8 0.6 select_reduce_fusion.entry_of
  5.3 76.2 %exchange.1 = (f32[256,2048]{1,0:T(8,128)}, f32[256,2048]{1,0:T(8,128)}, bf16[4096,256]{1,0:T(8,128)(2,1)}, f32[256,128]{1,0:T(8,128)}) custom-call(s32[32]{0:T(128)} %get-tuple-element.23.take_first, s32[32]{0:T(128)} %get-tuple-element.22.take_second, s32[32]{0:T(128)} %get-tuple-element.24.slot_of, s32[33]{0:T(128)} %select_reduce_fusion.entry_of, ...), custom_call_target="tpu_custom_call" | custom-call | tf_op jit(solution)/shard_map/exchange/pallas_call | solution.py:284
  81.5 12.3 %gradients.1 = (bf16[256,2048]{1,0:T(8,128)(2,1)}, bf16[4096,2048]{1,0:T(8,128)(2,1)}, f32[1,1]{1,0:T(1,128)}) custom-call(f32[256,128]{1,0:T(8,128)} %get-tuple-element.10.cols_ref, f32[256,2048]{1,0:T(8,128)} %get-tuple-element.11.logits_ref, f32[256,2048]{1,0:T(8,128)} %get-tuple-element.12.mapped_ref, bf16[4096,256]{1,0:T(8,128)(2,1)} %get-tuple-element.13.turned_ref), custom_call_target="tpu_custom_call" | custom-call | tf_op jit(solution)/shard_map/gradients/pallas_call | solution.py:357
  (5 shorter events, 0.1 us)
